TPU v7x, 32 devices: a whole 2x2x4 slice. The times are simulated.
32 devices in a mesh: row: 2 (over core), col: 4 (over z), dp: 4 (over y, x).
Axes of the slice: x: 2, y: 2, z: 4, core: 2. Of those that a mesh axis runs over, the one named last changes fastest.
Arguments:
- activations: bfloat16 [4, 256, 16384], P('dp', 'col', 'row'), may hold values from -6 to 6
- out_grads: bfloat16 [4, 256, 4096], P('dp', 'row', 'col'), may hold values from -6 to 6
- block_mask: int32 [128, 32], P('row', 'col'), may hold values from 0 to 1, as said below
- master_weight: float32 [16384, 4096], P(('row', 'dp'), 'col'), may hold values from -0.046875 to 0.046875
- first_moment: float32 [16384, 4096], P(('row', 'dp'), 'col'), may hold values from -12 to 12
- second_moment: float32 [16384, 4096], P(('row', 'dp'), 'col'), may hold values from 0.05 to 2
Outputs:
- input_grads: bfloat16 [4, 256, 16384], P('dp', 'col', 'row')
- new_weight: float32 [16384, 4096], P(('row', 'dp'), 'col')
- new_first: float32 [16384, 4096], P(('row', 'dp'), 'col')
- new_second: float32 [16384, 4096], P(('row', 'dp'), 'col')
Inputs may be any that keep to these rules, and one draw needn't show every extreme that they name: `block_mask`: 1 where the 128 x 128 block of the weight is kept, 0 where it is pruned.
All inputs are finite; a program needn't handle non-finite values.
Results may differ from a plain program's by a relative error of at most 0.015.
Values may be sent and summed in bfloat16 or wider, within the bound.
A program may use at most 192 MiB of HBM per device.

v0:
```python
import jax
import jax.numpy as jnp
from jax import lax
from jax.sharding import PartitionSpec as P

BLOCK = 128


first_decay = 0.9
second_decay = 0.999
learn_rate = 0.001
adam_epsilon = 1e-08
first_correct = 1.0 - 0.9**10
second_correct = 1.0 - 0.999**10


def expand(block_keep):
    tall, broad = block_keep.shape
    values = block_keep.astype(jnp.float32)
    grown = jnp.broadcast_to(values[:, None, :, None], (tall, BLOCK, broad, BLOCK))
    return grown.reshape(tall * BLOCK, broad * BLOCK)


def body(activations, out_grads, block_mask, master_weight, first_moment, second_moment):
    shard_rows = master_weight.shape[0]
    group_index = lax.axis_index("dp")
    keep_tile = expand(block_mask)
    keep_shard = lax.dynamic_slice_in_dim(keep_tile, group_index * shard_rows, shard_rows, 0)
    weight_tile = lax.all_gather(master_weight.astype(jnp.bfloat16), "dp", axis=0, tiled=True)
    weight_tile = weight_tile * keep_tile.astype(jnp.bfloat16)
    grad_group = lax.all_gather(out_grads[0], "row", axis=0, tiled=True)
    picked = grad_group
    summed_inputs = lax.psum_scatter(
        lax.dot_general(
            picked, weight_tile, (((1,), (1,)), ((), ())), preferred_element_type=jnp.float32
        ).astype(jnp.bfloat16),
        "col",
        scatter_dimension=0,
        tiled=True,
    ).astype(jnp.float32)
    summed_inputs, acts_after = lax.optimization_barrier((summed_inputs, activations[0]))
    picked = grad_group
    tile_grad = (
        lax.dot_general(
            lax.all_gather(acts_after, "col", axis=0, tiled=True),
            picked,
            (((0,), (0,)), ((), ())),
            preferred_element_type=jnp.float32,
        )
        * keep_tile
    )
    input_grads = summed_inputs.astype(jnp.bfloat16)[None]
    grad_shard = lax.psum_scatter(
        tile_grad.astype(jnp.bfloat16), "dp", scatter_dimension=0, tiled=True
    ).astype(jnp.float32)
    new_first = first_decay * first_moment + (1.0 - first_decay) * grad_shard
    new_second = second_decay * second_moment + (1.0 - second_decay) * grad_shard * grad_shard
    step_size = new_first / first_correct / (jnp.sqrt(new_second / second_correct) + adam_epsilon)
    new_weight = keep_shard * (master_weight - learn_rate * step_size)
    return (input_grads, new_weight, new_first, new_second)


def solution(mesh):
    return jax.shard_map(
        body,
        mesh=mesh,
        in_specs=(
            P("dp", "col", "row"),
            P("dp", "row", "col"),
            P("row", "col"),
            P(("row", "dp"), "col"),
            P(("row", "dp"), "col"),
            P(("row", "dp"), "col"),
        ),
        out_specs=(
            P("dp", "col", "row"),
            P(("row", "dp"), "col"),
            P(("row", "dp"), "col"),
            P(("row", "dp"), "col"),
        ),
        check_vma=False,
    )
```

profile of v0, /device:TPU:0, one launch (start us, length us, event | category | flops | bytes accessed | tf_op | source)
XLA Modules:
  0.0 581.8 jit_solution(16110771003988277990)
XLA Ops:
  7.2 0.0 copy-start.1
  7.2 0.0 copy-start
  7.2 0.0 all-gather.4.cloned.1.call-start
  7.2 6.1 %convert_element_type.27 = bf16[2048,1024]{1,0:T(8,128)(2,1)} convert(f32[2048,1024]{1,0:T(8,128)} %param.9) | non-fusion elementwise | flops 2097152 | bytes 12582912 | tf_op jit(solution)/shard_map/convert_element_type | solution.py:29
  13.3 0.0 all-gather.4.cloned.1.call-update
  13.4 0.0 reduce-scatter.7.cloned.1.call-start
  13.4 0.0 copy-done.1
  13.4 0.1 copy.12
  13.5 0.0 copy-done
  13.5 2.3 all-gather
  15.8 157.7 %all-gather.4.cloned.1.call-done = bf16[8192,1024]{1,0:T(8,128)(2,1)} async-done(((bf16[2048,1024]{1,0:T(8,128)(2,1)}), bf16[8192,1024]{1,0:T(8,128)(2,1)}) %all-gather.4.cloned.1.call-update) | async-done | bytes 16777232 | tf_op jit(solution)/shard_map/all_gather | solution.py:29
  173.5 11.1 %broadcast_in_dim.4 = f32[64,128,8,128]{3,2,1,0:T(8,128)} broadcast(f32[64,8]{1,0:T(8,128)S(1)} %copy.12), dimensions={0,2} | broadcast | bytes 33556480 | tf_op jit(solution)/shard_map/broadcast_in_dim | solution.py:20
  184.6 22.8 %fusion.6 = bf16[256,8192]{0,1:T(8,128)(2,1)} fusion(bf16[8192,1024]{1,0:T(8,128)(2,1)} %all-gather.4.cloned.1.call-done, bf16[1,256,1024]{2,1,0:T(8,128)(2,1)S(1)} %all-gather, f32[1024,8,8,128]{3,2,1,0:T(8,128)} %bitcast.23), kind=kOutput, calls=%fused_computation.8 | convolution fusion | flops 4305453056 | bytes 55050240 | tf_op jit(solution)/shard_map/dot_general | solution.py:34
  207.4 6.3 %copy.14 = bf16[256,8192]{1,0:T(8,128)(2,1)} copy(bf16[256,8192]{0,1:T(8,128)(2,1)} %fusion.6) | data formatting | bytes 8388608
  213.7 0.0 reduce-scatter.7.cloned.1.call-update
  213.7 0.0 all-gather.6.cloned.1.call-start
  213.8 76.9 %reduce-scatter.7.cloned.1.call-done = bf16[64,8192]{1,0:T(8,128)(2,1)} async-done(((bf16[256,8192]{1,0:T(8,128)(2,1)}), bf16[64,8192]{1,0:T(8,128)(2,1)}) %reduce-scatter.7.cloned.1.call-update) | async-done | bytes 1048592
  290.7 2.0 copy.15
  292.7 0.0 all-gather.6.cloned.1.call-update
  292.7 0.2 reduce-scatter.5.cloned.1.call-start
  293.0 81.2 %all-gather.6.cloned.1.call-done = bf16[256,8192]{1,0:T(8,128)(2,1)} async-done(((bf16[64,8192]{1,0:T(8,128)(2,1)}), bf16[256,8192]{1,0:T(8,128)(2,1)}) %all-gather.6.cloned.1.call-update) | async-done | bytes 4194320 | tf_op jit(solution)/shard_map/all_gather | solution.py:45
  374.1 24.9 %multiply_convert_fusion = bf16[8192,1024]{1,0:T(8,128)(2,1)} fusion(bf16[256,8192]{1,0:T(8,128)(2,1)} %all-gather.6.cloned.1.call-done, bf16[1,256,1024]{2,1,0:T(8,128)(2,1)S(1)} %all-gather, f32[1024,8,8,128]{3,2,1,0:T(8,128)} %bitcast.24), kind=kOutput, calls=%fused_computation.1 | convolution fusion | flops 4311744512 | bytes 55050240 | tf_op jit(solution)/shard_map/dot_general | solution.py:44
  399.0 0.0 reduce-scatter.5.cloned.1.call-update
  399.0 27.9 %copy.23 = f32[1024,8,8,128]{3,1,2,0:T(8,128)} copy(f32[1024,8,8,128]{3,2,1,0:T(8,128)} %bitcast.25) | data formatting | bytes 67108864
  426.9 1.6 copy.13
  428.5 122.9 %reduce-scatter.5.cloned.1.call-done = bf16[2048,1024]{1,0:T(8,128)(2,1)} async-done(((bf16[8192,1024]{1,0:T(8,128)(2,1)}), bf16[2048,1024]{1,0:T(8,128)(2,1)}) %reduce-scatter.5.cloned.1.call-update) | async-done | bytes 4194320 | tf_op jit(solution)/shard_map/reduce_scatter | solution.py:53
  551.4 23.9 %subtract_multiply_fusion = (f32[2048,1024]{1,0:T(8,128)}, f32[2048,1024]{1,0:T(8,128)}, f32[2048,1024]{1,0:T(8,128)}) fusion(f32[2048,1024]{1,0:T(8,128)} %param.9, f32[8192,1024]{1,0:T(8,128)} %bitcast.26, s32[]{:T(128)S(6)} %select_n.3, bf16[2048,1024]{1,0:T(8,128)(2,1)} %reduce-scatter.5.cloned.1.call-done, f32[2048,1024]{1,0:T(8,128)} %param.10, ...), kind=kLoop, calls=%fused_computation.11 | loop fusion | flops 31457280 | bytes 62914564 | tf_op jit(solution)/shard_map/mul | solution.py:59
  (1 shorter events, 0.0 us)
Async XLA Ops:
  7.2 6.2 %copy-start.1 = (s32[64,8]{0,1:T(8,128)S(1)}, s32[64,8]{0,1:T(8,128)}, u32[]{:S(2)}) copy-start(s32[64,8]{0,1:T(8,128)} %param.8) | copy-start | bytes 6148
  7.2 6.3 %copy-start = (bf16[1,128,1024]{2,1,0:T(8,128)(2,1)S(1)}, bf16[1,128,1024]{2,1,0:T(8,128)(2,1)}, u32[]{:S(2)}) copy-start(bf16[1,128,1024]{2,1,0:T(8,128)(2,1)} %param.7) | copy-start | bytes 786436
  7.2 166.3 %all-gather.4.cloned.1.call-start = ((), (), s32[]{:S(2)}) async-start(), calls=%async_computation.2 | async-start | bytes 20971520 | tf_op jit(solution)/shard_map/all_gather | solution.py:29
  13.4 277.3 %reduce-scatter.7.cloned.1.call-start = ((), (), s32[]{:S(2)}) async-start(), calls=%async_computation.5 | async-start | bytes 5242880
  213.7 160.4 %all-gather.6.cloned.1.call-start = ((), (), s32[]{:S(2)}) async-start(), calls=%async_computation.3 | async-start | bytes 5242880 | tf_op jit(solution)/shard_map/all_gather | solution.py:45
  292.7 258.7 %reduce-scatter.5.cloned.1.call-start = ((), (), s32[]{:S(2)}) async-start(), calls=%async_computation.4 | async-start | bytes 20971520 | tf_op jit(solution)/shard_map/reduce_scatter | solution.py:53
Sparse Core Ops, SparseCore 0:
  13.5 160.0 all-gather.3
  213.8 76.7 reduce-scatter.6
  292.9 81.2 all-gather.5
  399.2 152.1 reduce-scatter.4
where the time goes:
time: 582 us
  waiting for transfers between devices  439 us (75%)
  local copies, waits for them, and re-layouts  49 us (8%)
  matrix products  47.7 us (8%)
  other arithmetic  30 us (5%)
  between operations  13.8 us (2%)
    all_gather x1, waiting for transfers between devices, body(): lax.all_gather(master_weight.astype(jnp.bfloat16), 'dp', axis=0, tiled=True)  158 us
    reduce_scatter x1, waiting for transfers between devices, body(): lax.psum_scatter(tile_grad.astype(jnp.bfloat16), 'dp', scatter_dimension=...  123 us
    all_gather x1, waiting for transfers between devices, body(): lax.all_gather(acts_after, 'col', axis=0, tiled=True)  81.2 us
    unnamed x5, waiting for transfers between devices  77 us
    unnamed x7, local copies, waits for them, and re-layouts  35.8 us
    dot_general x1, matrix products, body(): lax.dot_general(lax.all_gather(acts_after, 'col', axis=0, tiled=True), pi...  24.9 us
    mul x1, other arithmetic, body(): new_weight = keep_shard * (master_weight - learn_rate * step_size)  23.9 us
    dot_general x1, matrix products, body(): lax.dot_general(picked, weight_tile, (((1,), (1,)), ((), ())), preferred_...  22.8 us
  transfers between devices with their start and end apart: 4, of which 4 were waited for; matrix products, arithmetic and copies ran while one was open for 5% of the time, Pallas kernels for 0%

commit v1 on v0

v1 whole, which is shorter than its diff:
```python
import jax
import jax.numpy as jnp
from jax import lax
from jax.sharding import PartitionSpec as P

BLOCK = 128


first_decay = 0.9
second_decay = 0.999
learn_rate = 0.001
adam_epsilon = 1e-08
first_correct = 1.0 - 0.9**10
second_correct = 1.0 - 0.999**10


def expand(block_keep):
    tall, broad = block_keep.shape
    values = block_keep.astype(jnp.float32)
    grown = jnp.broadcast_to(values[:, None, :, None], (tall, BLOCK, broad, BLOCK))
    return grown.reshape(tall * BLOCK, broad * BLOCK)


def body(activations, out_grads, block_mask, master_weight, first_moment, second_moment):
    groups = lax.axis_size("dp")
    cols = lax.axis_size("col")
    shard_rows, shard_cols = master_weight.shape
    part = activations.shape[1]
    shard_blocks = shard_rows // BLOCK
    group_index = lax.axis_index("dp")
    keep_blocks = lax.dynamic_slice_in_dim(
        block_mask, group_index * shard_blocks, shard_blocks, 0
    )
    keep_shard = expand(keep_blocks)
    cotangents = lax.all_gather(out_grads[0], ("dp", "row"), axis=0, tiled=True)
    cotangents = (
        cotangents.reshape(groups, cols, part, shard_cols)
        .transpose(1, 0, 2, 3)
        .reshape(cols * groups * part, shard_cols)
    )
    acts = lax.all_to_all(activations[0], "dp", split_axis=1, concat_axis=0, tiled=True)
    acts = lax.all_gather(acts, "col", axis=0, tiled=True)
    pruned = master_weight.astype(jnp.bfloat16) * keep_shard.astype(jnp.bfloat16)
    partial = lax.dot_general(
        cotangents, pruned, (((1,), (1,)), ((), ())), preferred_element_type=jnp.float32
    ).astype(jnp.bfloat16)
    summed = lax.psum_scatter(partial, "col", scatter_dimension=0, tiled=True)
    summed = lax.all_to_all(summed, "dp", split_axis=0, concat_axis=1, tiled=True)
    input_grads = summed[None]
    grad_shard = (
        lax.dot_general(
            acts, cotangents, (((0,), (0,)), ((), ())), preferred_element_type=jnp.float32
        )
        * keep_shard
    )
    new_first = first_decay * first_moment + (1.0 - first_decay) * grad_shard
    new_second = second_decay * second_moment + (1.0 - second_decay) * grad_shard * grad_shard
    step_size = new_first / first_correct / (jnp.sqrt(new_second / second_correct) + adam_epsilon)
    new_weight = keep_shard * (master_weight - learn_rate * step_size)
    return (input_grads, new_weight, new_first, new_second)


def solution(mesh):
    return jax.shard_map(
        body,
        mesh=mesh,
        in_specs=(
            P("dp", "col", "row"),
            P("dp", "row", "col"),
            P("row", "col"),
            P(("row", "dp"), "col"),
            P(("row", "dp"), "col"),
            P(("row", "dp"), "col"),
        ),
        out_specs=(
            P("dp", "col", "row"),
            P(("row", "dp"), "col"),
            P(("row", "dp"), "col"),
            P(("row", "dp"), "col"),
        ),
        check_vma=False,
    )
```

time: 582 us -> 248 us (0.43)
  waiting for transfers between devices: 439 us -> 166 us
  local copies, waits for them, and re-layouts: 49 us -> 12.8 us
  other arithmetic: 30 us -> 0.76 us
  blocking collectives: 2.3 us -> 18 us
  matrix products: 47.7 us -> 32.9 us
    all_gather x2, waiting for transfers between devices: 239 us -> 109 us  [the longest x1 77 us: body(): acts = lax.all_gather(acts, 'col', axis=0, tiled=True)]
    unnamed x5 -> x3, waiting for transfers between devices: 77 us -> 0.71 us
    reduce_scatter x1, waiting for transfers between devices: 123 us -> 56.5 us  [body(): summed = lax.psum_scatter(partial, 'col', scatter_dimension=0, tiled=True)]
    unnamed x7 -> x2, local copies, waits for them, and re-layouts: 35.8 us -> 3.22 us
    mul x1 -> x0, other arithmetic: 23.9 us -> none  [body(): new_weight = keep_shard * (master_weight - learn_rate * step_size)]
    all_to_all x0 -> x1, blocking collectives: none -> 18 us  [body(): lax.all_to_all(activations[0], 'dp', split_axis=1, concat_axis=0, tiled=T...]
    dot_general x2, matrix products: 47.7 us -> 32.9 us  [the longest x1 23.1 us: body(): lax.dot_general(acts, cotangents, (((0,), (0,)), ((), ())), preferred_ele...]
    broadcast_in_dim x1, local copies, waits for them, and re-layouts: 11.1 us -> 0.6 us  [expand(): jnp.broadcast_to(values[:, None, :, None], (tall, BLOCK, broad, BLOCK))]
  transfers between devices with their start and end apart: 4 -> 4, of which waited for: 4 -> 3; matrix products, arithmetic and copies ran while one was open for 5% -> 11% of each run, Pallas kernels for 0% -> 0%
where the time goes in v1:
time: 248 us
  waiting for transfers between devices  166 us (67%)
  matrix products  32.9 us (13%)
  blocking collectives  18 us (7%)
  between operations  13.8 us (6%)
  local copies, waits for them, and re-layouts  12.8 us (5%)
  starting transfers between devices  3.74 us (2%)
    all_gather x1, waiting for transfers between devices, body(): acts = lax.all_gather(acts, 'col', axis=0, tiled=True)  77 us
    reduce_scatter x1, waiting for transfers between devices, body(): summed = lax.psum_scatter(partial, 'col', scatter_dimension=0, tiled=True)  56.5 us
    all_gather x1, waiting for transfers between devices, body(): cotangents = lax.all_gather(out_grads[0], ('dp', 'row'), axis=0, tiled=True)  31.6 us
    dot_general x1, matrix products, body(): lax.dot_general(acts, cotangents, (((0,), (0,)), ((), ())), preferred_ele...  23.1 us
    all_to_all x1, blocking collectives, body(): lax.all_to_all(activations[0], 'dp', split_axis=1, concat_axis=0, tiled=T...  18 us
    dot_general x1, matrix products, body(): lax.dot_general(cotangents, pruned, (((1,), (1,)), ((), ())), preferred_e...  9.84 us
  transfers between devices with their start and end apart: 4, of which 3 were waited for; matrix products, arithmetic and copies ran while one was open for 11% of the time, Pallas kernels for 0%

profile of v1, /device:TPU:0, one launch (start us, length us, event | category | flops | bytes accessed | tf_op | source)
XLA Modules:
  0.0 247.7 jit_solution(3966970506751093546)
XLA Ops:
  7.2 0.0 all-gather.6.cloned.1.call-start
  7.2 0.7 all-gather.6.cloned.1.call-update
  7.9 0.0 reduce-scatter.2.cloned.1.call-start
  7.9 0.8 dynamic-slice_convert_fusion
  8.7 0.1 copy.19
  8.8 31.6 %all-gather.6.cloned.1.call-done = bf16[1,1024,1024]{2,1,0:T(8,128)(2,1)} async-done(((bf16[1,128,1024]{2,1,0:T(8,128)(2,1)}), bf16[1,1024,1024]{2,1,0:T(8,128)(2,1)}) %all-gather.6.cloned.1.call-update) | async-done | bytes 2097168 | tf_op jit(solution)/shard_map/all_gather | solution.py:35
  40.4 1.8 copy.20
  42.2 0.6 broadcast_in_dim.4
  42.8 0.0 copy-start
  42.8 3.2 %copy-done = f32[16,128,8,128]{3,2,1,0:T(8,128)} copy-done((f32[16,128,8,128]{3,2,1,0:T(8,128)}, f32[16,128,8,128]{3,2,1,0:T(8,128)S(1)}, u32[]{:S(2)}) %copy-start) | copy-done | bytes 8388632
  46.1 9.8 %convert_bitcast_fusion = bf16[1024,2048]{0,1:T(8,128)(2,1)} fusion(bf16[1024,1024]{1,0:T(8,128)(2,1)S(1)} %bitcast.29, f32[256,8,8,128]{3,2,1,0:T(8,128)S(1)} %bitcast.25, f32[2048,1024]{1,0:T(8,128)} %param.9), kind=kOutput, calls=%fused_computation.8 | convolution fusion | flops 4301258752 | bytes 23068672 | tf_op jit(solution)/shard_map/dot_general | solution.py:44
  55.9 0.0 reduce-scatter.2.cloned.1.call-update
  55.9 0.0 all-gather.4.cloned.1.call-start
  56.0 1.8 all_to_all.29
  57.8 0.6 copy.23
  58.4 18.0 %all_to_all.35 = bf16[64,4,2048]{2,0,1:T(8,128)(2,1)} all-to-all(bf16[64,4,2048]{2,0,1:T(8,128)(2,1)S(1)} %copy.23), channel_id=1, replica_groups=mesh['row'=2,'col'=4,'dp'=4] {'dp'}, dimensions={1} | all-to-all | bytes 2097152 | tf_op jit(solution)/shard_map/all_to_all | solution.py:41
  76.4 0.0 all-gather.4.cloned.1.call-update
  76.4 56.5 %reduce-scatter.2.cloned.1.call-done = bf16[256,2048]{0,1:T(8,128)(2,1)} async-done(((bf16[1024,2048]{0,1:T(8,128)(2,1)}), bf16[256,2048]{0,1:T(8,128)(2,1)}) %reduce-scatter.2.cloned.1.call-update) | async-done | bytes 1048592 | tf_op jit(solution)/shard_map/reduce_scatter | solution.py:47
  132.9 2.3 copy.21
  135.1 3.6 %all-to-all-start = ((bf16[4,64,2048]{2,1,0:T(8,128)(2,1)}), bf16[4,64,2048]{2,1,0:T(8,128)(2,1)S(1)}, u32[]{:S(2)}, u32[]{:S(2)}) async-start(bf16[4,64,2048]{2,1,0:T(8,128)(2,1)} %bitcast.4), calls=%async_computation.1 | async-start | bytes 2097152 | tf_op jit(solution)/shard_map/all_to_all | solution.py:48
  138.8 77.0 %all-gather.4.cloned.1.call-done = bf16[1024,2048]{1,0:T(8,128)(2,1)} async-done(((bf16[256,2048]{1,0:T(8,128)(2,1)}), bf16[1024,2048]{1,0:T(8,128)(2,1)}) %all-gather.4.cloned.1.call-update) | async-done | bytes 4194320 | tf_op jit(solution)/shard_map/all_gather | solution.py:42
  215.7 23.1 %bitcast_multiply_fusion = (f32[2048,1024]{1,0:T(8,128)}, f32[2048,1024]{1,0:T(8,128)}, f32[2048,1024]{1,0:T(8,128)}) fusion(f32[2048,1024]{1,0:T(8,128)} %param.9, f32[256,8,8,128]{3,2,1,0:T(8,128)} %bitcast.26, f32[2048,1024]{1,0:T(8,128)} %param.10, f32[2048,1024]{1,0:T(8,128)} %param.11, bf16[1024,2048]{1,0:T(8,128)(2,1)} %all-gather.4.cloned.1.call-done, ...), kind=kOutput, calls=%fused_computation.2 | convolution fusion | flops 4326424576 | bytes 65011712 | tf_op jit(solution)/shard_map/dot_general | solution.py:51
  238.8 0.0 all-to-all-done
  238.8 0.8 copy.22
  239.6 1.6 broadcast_in_dim.10
Async XLA Ops:
  7.2 33.2 %all-gather.6.cloned.1.call-start = ((), (), s32[]{:S(2)}) async-start(), calls=%async_computation.5 | async-start | bytes 2359296 | tf_op jit(solution)/shard_map/all_gather | solution.py:35
  7.9 125.0 %reduce-scatter.2.cloned.1.call-start = ((), (), s32[]{:S(2)}) async-start(), calls=%async_computation.3 | async-start | bytes 5242880 | tf_op jit(solution)/shard_map/reduce_scatter | solution.py:47
  42.8 3.2 %copy-start = (f32[16,128,8,128]{3,2,1,0:T(8,128)}, f32[16,128,8,128]{3,2,1,0:T(8,128)S(1)}, u32[]{:S(2)}) copy-start(f32[16,128,8,128]{3,2,1,0:T(8,128)S(1)} %broadcast_in_dim.4) | copy-start | bytes 25165828
  55.9 159.8 %all-gather.4.cloned.1.call-start = ((), (), s32[]{:S(2)}) async-start(), calls=%async_computation.4 | async-start | bytes 5242880 | tf_op jit(solution)/shard_map/all_gather | solution.py:42
  135.1 103.6 %all-to-all-start = ((bf16[4,64,2048]{2,1,0:T(8,128)(2,1)}), bf16[4,64,2048]{2,1,0:T(8,128)(2,1)S(1)}, u32[]{:S(2)}, u32[]{:S(2)}) async-start(bf16[4,64,2048]{2,1,0:T(8,128)(2,1)} %bitcast.4), calls=%async_computation.1 | async-start | bytes 2097152 | tf_op jit(solution)/shard_map/all_to_all | solution.py:48
Sparse Core Ops, SparseCore 0:
  9.9 30.4 all-gather.5
  56.0 76.7 reduce-scatter.1
  134.5 81.2 all-gather.3
